TPU v7x, 256 devices: a whole 4x4x8 slice. The times are simulated.
256 devices in a mesh: layer: 8 (over x, y_hi), feat: 32 (over y_lo, z, core).
Axes of the slice: x: 4, y: 4 (y_hi: 2, y_lo: 2; y = y_hi * 2 + y_lo), z: 8, core: 2. Of those that a mesh axis runs over, the one named last changes fastest.
Arguments:
- inputs: bfloat16 [8, 512, 2048], P('layer', 'feat'), may hold values from -6 to 6
- targets: bfloat16 [8, 512, 2048], P('layer', 'feat'), may hold values from -6 to 6
- enc_weight: bfloat16 [8, 2048, 16384], P('layer', None, 'feat'), may hold values from -0.125 to 0.125
- enc_bias: float32 [8, 16384], P('layer', 'feat'), may hold values from -1 to 0.5
- dec_weight: bfloat16 [8, 2, 16384, 2048], P('layer', None, 'feat'), may hold values from -0.046875 to 0.046875
- dec_bias: float32 [8, 2048], P('layer'), may hold values from -3 to 3
Outputs:
- mean_loss: float32 [], replicated
- enc_grad: bfloat16 [8, 2048, 16384], P('layer', None, 'feat')
- enc_bias_grad: float32 [8, 16384], P('layer', 'feat')
- dec_grad: bfloat16 [8, 2, 16384, 2048], P('layer', None, 'feat')
- dec_bias_grad: float32 [8, 2048], P('layer')
All inputs are finite; a program needn't handle non-finite values.
Results may differ from a plain program's by a relative error of at most 0.006.
Values may be sent and summed in bfloat16 or wider, within the bound.
A program may use at most 128 MiB of HBM per device.

v0:
```python
import functools
import jax
import jax.numpy as jnp
from jax import lax
from jax.sharding import Mesh
from jax.sharding import PartitionSpec as P

FEAT = ("feat_0", "feat_1", "feat_2")
LAYER = ("layer_0", "layer_1")
LAYER_FEAT = ("layer_0", "layer_1", "feat_0", "feat_1", "feat_2")


def copy_for_each(value, axis):
    size = lax.axis_size(axis)
    return lax.all_to_all(
        jnp.broadcast_to(value[None], (size, *value.shape)), axis, 0, 0, tiled=True
    )


def joined_along(tiles, dim):
    lengths = list(tiles.shape[1:])
    lengths[dim] *= tiles.shape[0]
    return jnp.moveaxis(tiles, 0, dim).reshape(lengths)


def collect(value, axis, dim):
    tiles = copy_for_each(value, axis)
    return joined_along(tiles, dim)


def cut_along(value, dim, size):
    lengths = value.shape
    tiles = value.reshape(*lengths[:dim], size, lengths[dim] // size, *lengths[dim + 1 :])
    return jnp.moveaxis(tiles, dim, 0)


def scatter_pairs(value, chips, core, dim):
    sizes = (lax.axis_size(chips), lax.axis_size(core))
    tiles = cut_along(value, dim, sizes[0] * sizes[1])
    inside = tiles.shape[1:]
    tiles = tiles.reshape(*sizes, *inside).swapaxes(0, 1).reshape(-1, *inside)
    tiles = lax.psum_scatter(tiles, core, scatter_dimension=0, tiled=True)
    return lax.psum_scatter(tiles, chips, scatter_dimension=0, tiled=True)[0]


def passed_along(block, axis, distance):
    devices = range(lax.axis_size(axis))
    route = [(i - distance, i) for i in devices if i - distance in devices]
    return lax.ppermute(block, axis, route)


def one_axis_at_a_time(value, axes):
    return functools.reduce(lax.psum, axes, value)


def shards(inputs, targets, enc_weight, enc_bias, dec_weight, dec_bias):
    shard_rows = inputs.shape[1]
    reach = dec_weight.shape[1]
    width = dec_weight.shape[3]
    tokens_all = collect(inputs[0], FEAT, 0)
    pre = jnp.dot(tokens_all, enc_weight[0], preferred_element_type=jnp.float32) + enc_bias[0]
    acts = (jnp.maximum(pre, 0.0) ** 2).astype(jnp.bfloat16)
    out = jnp.einsum("tf,rfd->trd", acts, dec_weight[0], preferred_element_type=jnp.float32)
    summed = scatter_pairs(
        out.reshape(
            shard_rows * lax.axis_size(("feat_0", "feat_1")) * lax.axis_size("feat_2"),
            reach * width,
        ),
        ("feat_0", "feat_1"),
        "feat_2",
        0,
    )
    recon = summed[:, :width] + dec_bias[0]
    offset = 1
    recon = recon + passed_along(summed[:, offset * width : (offset + 1) * width], LAYER, offset)
    grad = (recon - targets[0].astype(jnp.float32)).astype(jnp.bfloat16)
    local_squares = jnp.sum(grad.astype(jnp.float32) ** 2)
    total = one_axis_at_a_time(local_squares, LAYER_FEAT)
    mean_loss = total / (lax.axis_size(LAYER) * lax.axis_size(FEAT) * shard_rows * width)
    pieces = [grad]
    offset = 1
    pieces.append(passed_along(grad, LAYER, -offset))
    stacked = jnp.stack(pieces, axis=1)
    gathered = lax.all_gather(stacked, FEAT, axis=0, tiled=True)
    fulls = [gathered[:, offset] for offset in range(reach)]
    dec_parts = []
    back = jnp.zeros(pre.shape, jnp.float32)
    for offset in range(reach):
        dec_parts.append(
            jnp.einsum("tf,td->fd", acts, fulls[offset], preferred_element_type=jnp.float32).astype(
                jnp.bfloat16
            )
        )
        back = back + jnp.einsum(
            "td,fd->tf", fulls[offset], dec_weight[0, offset], preferred_element_type=jnp.float32
        )
    dec_grad = jnp.stack(dec_parts, axis=0)
    dpre = (back * 2.0 * jnp.maximum(pre, 0.0)).astype(jnp.bfloat16)
    enc_grad = jnp.einsum("td,tf->df", tokens_all, dpre, preferred_element_type=jnp.float32).astype(
        jnp.bfloat16
    )
    enc_bias_grad = jnp.sum(dpre.astype(jnp.float32), axis=0)
    dec_bias_grad = jnp.sum(fulls[0].astype(jnp.float32), axis=0)
    return (mean_loss, enc_grad[None], enc_bias_grad[None], dec_grad[None], dec_bias_grad[None])


def solution(mesh):
    finer = Mesh(
        mesh.devices.reshape(4, 2, 2, 8, 2), ("layer_0", "layer_1", "feat_0", "feat_1", "feat_2")
    )
    placed = (
        P(LAYER, FEAT, None),
        P(LAYER, FEAT, None),
        P(LAYER, None, FEAT),
        P(LAYER, FEAT),
        P(LAYER, None, FEAT, None),
        P(LAYER, None),
    )
    return jax.shard_map(
        shards,
        mesh=finer,
        in_specs=placed,
        out_specs=(
            P(),
            P(LAYER, None, FEAT),
            P(LAYER, FEAT),
            P(LAYER, None, FEAT, None),
            P(LAYER, None),
        ),
        check_vma=False,
    )
```

profile of v0, /device:TPU:1, one launch (start us, length us, event | category | flops | bytes accessed | tf_op | source)
XLA Modules:
  0.0 300.6 jit_solution(5352324902528373081)
XLA Ops:
  7.2 0.0 copy-start
  7.2 2.6 broadcast_in_dim.20
  9.7 11.2 %all-to-all-start = ((bf16[32,16,2048]{2,1,0:T(8,128)(2,1)}), bf16[32,16,2048]{2,1,0:T(8,128)(2,1)}, u32[]{:S(2)}, u32[]{:S(2)}) async-start(bf16[32,16,2048]{2,1,0:T(8,128)(2,1)} %broadcast_in_dim.20), calls=%async_computation | async-start | bytes 4194304 | tf_op jit(solution)/shard_map/all_to_all | solution.py:15
  20.9 0.0 copy-start.7
  20.9 0.0 reduce-scatter.3.cloned.1.call-start
  21.0 6.2 %copy.12 = bf16[1,2,512,2048]{2,3,1,0:T(8,128)(2,1)} copy(bf16[1,2,512,2048]{3,2,1,0:T(8,128)(2,1)} %param.10) | data formatting | bytes 8388608 | tf_op args[4]
  27.2 43.0 %all-to-all-done = bf16[32,16,2048]{2,1,0:T(8,128)(2,1)} async-done(((bf16[32,16,2048]{2,1,0:T(8,128)(2,1)}), bf16[32,16,2048]{2,1,0:T(8,128)(2,1)}, u32[]{:S(2)}, u32[]{:S(2)}) %all-to-all-start) | async-done | bytes 2097184 | tf_op jit(solution)/shard_map/all_to_all | solution.py:15
  70.2 0.0 copy-done
  70.2 0.0 copy-done.7
  70.2 0.0 copy-start.2
  70.2 4.0 %multiply_convert_fusion = (bf16[512,512]{1,0:T(8,128)(2,1)S(1)}, f32[512,512]{1,0:T(8,128)}) fusion(f32[512]{0:T(512)S(1)} %bitcast.97, bf16[512,2048]{1,0:T(8,128)(2,1)} %bitcast.1, bf16[1,2048,512]{2,1,0:T(8,128)(2,1)S(1)} %copy-done), kind=kOutput, calls=%fused_computation.26 | convolution fusion | flops 1074790400 | bytes 5769216 | tf_op jit(solution)/shard_map/dot_general | solution.py:61
  74.2 0.0 copy-done.2
  74.2 2.4 convolution_bitcast_fusion
  76.6 3.8 %copy.13 = f32[2,16,16,4096]{3,2,1,0:T(8,128)} copy(f32[2,16,16,4096]{3,2,0,1:T(8,128)S(1)} %convolution_bitcast_fusion) | data formatting | bytes 16777216 | tf_op jit(solution)/shard_map/transpose | solution.py:41
  80.4 0.0 reduce-scatter.3.cloned.1.call-update
  80.4 0.0 reduce-scatter.5.cloned.1.call-start
  80.5 21.5 %reduce-scatter.3.cloned.1.call-done = f32[16,16,4096]{2,1,0:T(8,128)} async-done(((f32[32,16,4096]{2,1,0:T(8,128)}), f32[16,16,4096]{2,1,0:T(8,128)}) %reduce-scatter.3.cloned.1.call-update) | async-done | bytes 4194320 | tf_op jit(solution)/shard_map/reduce_scatter | solution.py:42
  102.0 0.0 copy-start.5
  102.0 0.0 copy-start.6
  102.0 0.0 reduce-scatter.5.cloned.1.call-update
  102.0 0.0 all-gather.2.cloned.1.call-start
  102.1 74.0 %reduce-scatter.5.cloned.1.call-done = f32[1,16,4096]{2,1,0:T(8,128)} async-done(((f32[16,16,4096]{2,1,0:T(8,128)}), f32[1,16,4096]{2,1,0:T(8,128)}) %reduce-scatter.5.cloned.1.call-update) | async-done | bytes 262160 | tf_op jit(solution)/shard_map/reduce_scatter | solution.py:43
  176.0 0.9 slice.25
  176.9 4.4 %collective-permute-start = (f32[16,2048]{1,0:T(8,128)S(1)}, f32[16,2048]{1,0:T(8,128)S(1)}, u32[]{:S(2)}, u32[]{:S(2)}) collective-permute-start(f32[16,2048]{1,0:T(8,128)S(1)} %slice.25), channel_id=1, source_target_pairs={{0,32},{32,64},{64,96},{96,128},{128,160},{160,192},{192,224},{1,3... | collective-permute-start | bytes 393224 | tf_op jit(solution)/shard_map/ppermute | solution.py:49
  181.3 3.3 %collective-permute-done = f32[16,2048]{1,0:T(8,128)S(1)} collective-permute-done((f32[16,2048]{1,0:T(8,128)S(1)}, f32[16,2048]{1,0:T(8,128)S(1)}, u32[]{:S(2)}, u32[]{:S(2)}) %collective-permute-start) | collective-permute-done | bytes 131104 | tf_op jit(solution)/shard_map/ppermute | solution.py:49
  184.6 0.0 copy-done.5
  184.6 0.0 copy-done.6
  184.6 1.6 multiply_reduce_fusion
  186.2 1.3 collective-permute-start.1
  187.5 6.1 %collective-permute-done.1 = bf16[16,2048]{1,0:T(8,128)(2,1)S(1)} collective-permute-done((bf16[16,2048]{1,0:T(8,128)(2,1)S(1)}, bf16[16,2048]{1,0:T(8,128)(2,1)S(1)}, u32[]{:S(2)}, u32[]{:S(2)}) %collective-permute-start.1) | collective-permute-done | bytes 65568 | tf_op jit(solution)/shard_map/ppermute | solution.py:49
  193.5 0.7 pad_maximum_fusion
  194.2 0.0 all-gather.2.cloned.1.call-update
  194.2 9.7 %psum.35 = f32[]{:T(128)} all-reduce(f32[]{:T(128)} %get-tuple-element.15), channel_id=1, replica_groups=mesh['layer_0'=4,'layer_1'=2,'feat_0'=2,'feat_1'=8,'feat_2'=2] {'layer_0'}, use_global_device_ids=true, to_apply=%region_3.0 | all-reduce | flops 1 | bytes 8 | tf_op jit(solution)/shard_map/psum | solution.py:53
  203.9 5.9 %psum.36 = f32[]{:T(128)} all-reduce(f32[]{:T(128)} %psum.35), channel_id=1, replica_groups=mesh['layer_0'=4,'layer_1'=2,'feat_0'=2,'feat_1'=8,'feat_2'=2] {'layer_1'}, use_global_device_ids=true, to_apply=%region_4.0 | all-reduce | flops 1 | bytes 8 | tf_op jit(solution)/shard_map/psum | solution.py:53
  209.8 4.4 %psum.37 = f32[]{:T(128)} all-reduce(f32[]{:T(128)} %psum.36), channel_id=1, replica_groups=mesh['layer_0'=4,'layer_1'=2,'feat_0'=2,'feat_1'=8,'feat_2'=2] {'feat_0'}, use_global_device_ids=true, to_apply=%region_5.0 | all-reduce | flops 1 | bytes 8 | tf_op jit(solution)/shard_map/psum | solution.py:53
  214.2 11.8 %psum.38 = f32[]{:T(128)} all-reduce(f32[]{:T(128)} %psum.37), channel_id=1, replica_groups=mesh['layer_0'=4,'layer_1'=2,'feat_0'=2,'feat_1'=8,'feat_2'=2] {'feat_1'}, use_global_device_ids=true, to_apply=%region_6.0 | all-reduce | flops 1 | bytes 8 | tf_op jit(solution)/shard_map/psum | solution.py:53
  226.0 22.7 %psum.39 = f32[]{:T(128)} all-reduce(f32[]{:T(128)} %psum.38), channel_id=1, replica_groups=mesh['layer_0'=4,'layer_1'=2,'feat_0'=2,'feat_1'=8,'feat_2'=2] {'feat_2'}, use_global_device_ids=true, to_apply=%region_7.0 | all-reduce | flops 1 | bytes 8 | tf_op jit(solution)/shard_map/psum | solution.py:53
  249.4 20.9 %all-gather.2.cloned.1.call-done = bf16[512,2,2048]{2,0,1:T(8,128)(2,1)} async-done(((bf16[16,2,2048]{2,0,1:T(8,128)(2,1)}), bf16[512,2,2048]{2,0,1:T(8,128)(2,1)}) %all-gather.2.cloned.1.call-update) | async-done | bytes 4194320 | tf_op jit(solution)/shard_map/all_gather | solution.py:84
  270.3 0.0 copy-start.1
  270.3 0.0 copy-start.3
  270.3 0.0 copy-start.8
  270.3 3.7 %fusion.3 = f32[512,512]{1,0:T(8,128)S(1)} fusion(bf16[1,2,512,2048]{3,2,1,0:T(8,128)(2,1)} %param.10, bf16[512,2,2048]{2,0,1:T(8,128)(2,1)} %all-gather.2.cloned.1.call-done), kind=kOutput, calls=%fused_computation.11 | convolution fusion | flops 1073741824 | bytes 5242880 | tf_op jit(solution)/shard_map/td,fd->tf/dot_general | solution.py:94
  273.9 0.0 copy-done.1
  273.9 1.1 copy-done.3
  275.0 0.2 copy-done.8
  275.2 1.9 convert_reduce_fusion.1
  277.1 4.2 %fusion = bf16[1,2048,512]{1,2,0:T(8,128)(2,1)} fusion(bf16[512,512]{1,0:T(8,128)(2,1)S(1)} %get-tuple-element.20, bf16[512,2048]{1,0:T(8,128)(2,1)} %bitcast.1), kind=kOutput, calls=%fused_computation.6 | convolution fusion | flops 1074790400 | bytes 4718592 | tf_op jit(solution)/shard_map/td,tf->df/dot_general | solution.py:99
  281.3 3.9 %copy.14 = bf16[1,2048,512]{2,1,0:T(8,128)(2,1)} copy(bf16[1,2048,512]{1,2,0:T(8,128)(2,1)} %fusion) | data formatting | bytes 4194304
  285.2 0.0 copy-start.4
  285.2 3.0 %fusion.1 = bf16[1,512,2048]{2,1,0:T(8,128)(2,1)S(1)} fusion(bf16[512,512]{1,0:T(8,128)(2,1)S(1)} %get-tuple-element.17, bf16[512,2,2048]{2,0,1:T(8,128)(2,1)} %all-gather.2.cloned.1.call-done), kind=kOutput, calls=%fused_computation.7 | convolution fusion | flops 1074790400 | bytes 4718592 | tf_op jit(solution)/shard_map/tf,td->fd/dot_general | solution.py:90
  288.2 0.0 copy-done.4
  288.2 1.3 fusion.2
  289.5 2.4 maximum_bitcast_fusion
  291.9 1.0 convert_reduce_fusion
Async XLA Ops:
  7.2 63.1 %copy-start = (bf16[1,2048,512]{2,1,0:T(8,128)(2,1)S(1)}, bf16[1,2048,512]{2,1,0:T(8,128)(2,1)}, u32[]{:S(2)}) copy-start(bf16[1,2048,512]{2,1,0:T(8,128)(2,1)} %param.8) | copy-start | bytes 6291460
  9.7 60.5 %all-to-all-start = ((bf16[32,16,2048]{2,1,0:T(8,128)(2,1)}), bf16[32,16,2048]{2,1,0:T(8,128)(2,1)}, u32[]{:S(2)}, u32[]{:S(2)}) async-start(bf16[32,16,2048]{2,1,0:T(8,128)(2,1)} %broadcast_in_dim.20), calls=%async_computation | async-start | bytes 4194304 | tf_op jit(solution)/shard_map/all_to_all | solution.py:15
  20.9 49.3 %copy-start.7 = (f32[1,512]{1,0:T(1,128)S(1)}, f32[1,512]{1,0:T(1,128)}, u32[]{:S(2)}) copy-start(f32[1,512]{1,0:T(1,128)} %param.9) | copy-start | bytes 6148
  20.9 81.0 %reduce-scatter.3.cloned.1.call-start = ((), (), s32[]{:S(2)}) async-start(), calls=%async_computation.3 | async-start | bytes 12582912 | tf_op jit(solution)/shard_map/reduce_scatter | solution.py:42
  70.2 4.0 %copy-start.2 = (bf16[1,2,512,2048]{2,3,1,0:T(8,128)(2,1)S(1)}, bf16[1,2,512,2048]{2,3,1,0:T(8,128)(2,1)}, u32[]{:S(2)}) copy-start(bf16[1,2,512,2048]{2,3,1,0:T(8,128)(2,1)} %copy.12) | copy-start | bytes 12582916
  80.4 95.6 %reduce-scatter.5.cloned.1.call-start = ((), (), s32[]{:S(2)}) async-start(), calls=%async_computation.4 | async-start | bytes 4456448 | tf_op jit(solution)/shard_map/reduce_scatter | solution.py:43
  102.0 82.6 %copy-start.5 = (bf16[1,16,2048]{2,1,0:T(8,128)(2,1)S(1)}, bf16[1,16,2048]{2,1,0:T(8,128)(2,1)}, u32[]{:S(2)}) copy-start(bf16[1,16,2048]{2,1,0:T(8,128)(2,1)} %param.7) | copy-start | bytes 196612
  102.0 82.6 %copy-start.6 = (f32[1,2048]{1,0:T(1,128)S(1)}, f32[1,2048]{1,0:T(1,128)}, u32[]{:S(2)}) copy-start(f32[1,2048]{1,0:T(1,128)} %param.11) | copy-start | bytes 24580
  102.0 168.2 %all-gather.2.cloned.1.call-start = ((), (), s32[]{:S(2)}) async-start(), calls=%async_computation.5 | async-start | bytes 4325376 | tf_op jit(solution)/shard_map/all_gather | solution.py:84
  176.9 7.7 %collective-permute-start = (f32[16,2048]{1,0:T(8,128)S(1)}, f32[16,2048]{1,0:T(8,128)S(1)}, u32[]{:S(2)}, u32[]{:S(2)}) collective-permute-start(f32[16,2048]{1,0:T(8,128)S(1)} %slice.25), channel_id=1, source_target_pairs={{0,32},{32,64},{64,96},{96,128},{128,160},{160,192},{192,224},{1,3... | collective-permute-start | bytes 393224 | tf_op jit(solution)/shard_map/ppermute | solution.py:49
  186.2 7.4 %collective-permute-start.1 = (bf16[16,2048]{1,0:T(8,128)(2,1)S(1)}, bf16[16,2048]{1,0:T(8,128)(2,1)S(1)}, u32[]{:S(2)}, u32[]{:S(2)}) collective-permute-start(bf16[16,2048]{1,0:T(8,128)(2,1)S(1)} %get-tuple-element.16), channel_id=1, source_target_pairs={{32,0},{64,32},{96,64},{128,96},{160,128},{192,160},{224,192},{33,... | collective-permute-start | bytes 196616 | tf_op jit(solution)/shard_map/ppermute | solution.py:49
  270.3 3.7 %copy-start.1 = (bf16[1,2,512,2048]{3,2,1,0:T(8,128)(2,1)S(1)}, bf16[1,2,512,2048]{3,2,1,0:T(8,128)(2,1)}, u32[]{:S(2)}) copy-start(bf16[1,2,512,2048]{3,2,1,0:T(8,128)(2,1)} %param.10) | copy-start | bytes 12582916
  270.3 4.7 %copy-start.3 = (bf16[512,2,2048]{2,0,1:T(8,128)(2,1)S(1)}, bf16[512,2,2048]{2,0,1:T(8,128)(2,1)}, u32[]{:S(2)}) copy-start(bf16[512,2,2048]{2,0,1:T(8,128)(2,1)} %all-gather.2.cloned.1.call-done) | copy-start | bytes 12582916
  270.3 4.9 %copy-start.8 = (f32[512,512]{1,0:T(8,128)S(1)}, f32[512,512]{1,0:T(8,128)}, u32[]{:S(2)}) copy-start(f32[512,512]{1,0:T(8,128)} %get-tuple-element.18) | copy-start | bytes 3145732
  285.2 3.0 %copy-start.4 = (bf16[512,2,2048]{2,0,1:T(8,128)(2,1)S(1)}, bf16[512,2,2048]{2,0,1:T(8,128)(2,1)}, u32[]{:S(2)}) copy-start(bf16[512,2,2048]{2,0,1:T(8,128)(2,1)} %all-gather.2.cloned.1.call-done) | copy-start | bytes 12582916
Sparse Core Ops, SparseCore 0:
  80.5 21.3 reduce-scatter.2
  104.5 71.4 reduce-scatter.4
  194.4 75.8 all-gather.1
where the time goes:
time: 301 us
  waiting for transfers between devices  169 us (56%)
  blocking collectives  54.5 us (18%)
  matrix products  20.4 us (7%)
  local copies, waits for them, and re-layouts  18.7 us (6%)
  starting transfers between devices  17 us (6%)
  between operations  15.6 us (5%)
  other arithmetic  5.57 us (2%)
    reduce_scatter x1, waiting for transfers between devices, scatter_pairs(): return lax.psum_scatter(tiles, chips, scatter_dimension=0, tiled=True)[0]  74 us
    psum x5, blocking collectives, one_axis_at_a_time(): return functools.reduce(lax.psum, axes, value)  54.5 us
    all_to_all x1, waiting for transfers between devices, copy_for_each(): lax.all_to_all(jnp.broadcast_to(value[None], (size, *value.shape)), axis,...  43 us
    reduce_scatter x1, waiting for transfers between devices, scatter_pairs(): tiles = lax.psum_scatter(tiles, core, scatter_dimension=0, tiled=True)  21.5 us
    all_gather x1, waiting for transfers between devices, shards(): gathered = lax.all_gather(stacked, FEAT, axis=0, tiled=True)  20.9 us
    unnamed x20, local copies, waits for them, and re-layouts  11.4 us
    all_to_all x1, starting transfers between devices, copy_for_each(): lax.all_to_all(jnp.broadcast_to(value[None], (size, *value.shape)), axis,...  11.2 us
    ppermute x2, waiting for transfers between devices, passed_along(): return lax.ppermute(block, axis, route)  9.36 us
  transfers between devices with their start and end apart: 6, of which 6 were waited for; matrix products, arithmetic and copies ran while one was open for 2% of the time, Pallas kernels for 0%

commit v1 on v0

--- a/solution.py
+++ b/solution.py
@@ -81,7 +81,8 @@
     offset = 1
     pieces.append(passed_along(grad, LAYER, -offset))
     stacked = jnp.stack(pieces, axis=1)
-    gathered = lax.all_gather(stacked, FEAT, axis=0, tiled=True)
+    sent = jnp.stack([stacked] * lax.axis_size(FEAT))
+    gathered = jnp.concatenate(lax.all_to_all(sent, FEAT, 0, 0), axis=0)
     fulls = [gathered[:, offset] for offset in range(reach)]
     dec_parts = []
     back = jnp.zeros(pre.shape, jnp.float32)

time: 301 us -> 355 us (1.18)
  blocking collectives: 54.5 us -> 108 us
  waiting for transfers between devices: 169 us -> 148 us
  starting transfers between devices: 17 us -> 32.8 us
  local copies, waits for them, and re-layouts: 18.7 us -> 22.6 us
    psum x5, blocking collectives: 54.5 us -> 108 us  [one_axis_at_a_time(): return functools.reduce(lax.psum, axes, value)]
    all_gather x1 -> x0, waiting for transfers between devices: 20.9 us -> none  [shards(): gathered = lax.all_gather(stacked, FEAT, axis=0, tiled=True)]
    all_to_all x0 -> x1, starting transfers between devices: none -> 16.4 us  [shards(): gathered = jnp.concatenate(lax.all_to_all(sent, FEAT, 0, 0), axis=0)]
    unnamed x20 -> x16, local copies, waits for them, and re-layouts: 11.4 us -> 10.2 us
  transfers between devices with their start and end apart: 6 -> 6, of which waited for: 6 -> 5; matrix products, arithmetic and copies ran while one was open for 2% -> 2% of each run, Pallas kernels for 0% -> 0%
where the time goes in v1:
time: 355 us; the launch traced here: 354 us
  waiting for transfers between devices  148 us (42%)
  blocking collectives  108 us (30%)
  starting transfers between devices  32.8 us (9%)
  local copies, waits for them, and re-layouts  22.6 us (6%)
  matrix products  19 us (5%)
  between operations  15.9 us (4%)
  other arithmetic  7.16 us (2%)
    psum x5, blocking collectives, one_axis_at_a_time(): return functools.reduce(lax.psum, axes, value)  108 us
    reduce_scatter x1, waiting for transfers between devices, scatter_pairs(): return lax.psum_scatter(tiles, chips, scatter_dimension=0, tiled=True)[0]  74.1 us
    all_to_all x1, waiting for transfers between devices, copy_for_each(): lax.all_to_all(jnp.broadcast_to(value[None], (size, *value.shape)), axis,...  43 us
    reduce_scatter x1, waiting for transfers between devices, scatter_pairs(): tiles = lax.psum_scatter(tiles, core, scatter_dimension=0, tiled=True)  21.5 us
    all_to_all x1, starting transfers between devices, shards(): gathered = jnp.concatenate(lax.all_to_all(sent, FEAT, 0, 0), axis=0)  16.4 us
    all_to_all x1, starting transfers between devices, copy_for_each(): lax.all_to_all(jnp.broadcast_to(value[None], (size, *value.shape)), axis,...  11.2 us
    unnamed x16, local copies, waits for them, and re-layouts  10.2 us
    ppermute x2, waiting for transfers between devices, passed_along(): return lax.ppermute(block, axis, route)  9.36 us
  transfers between devices with their start and end apart: 6, of which 5 were waited for; matrix products, arithmetic and copies ran while one was open for 2% of the time, Pallas kernels for 0%

profile of v1, /device:TPU:1, one launch (start us, length us, event | category | flops | bytes accessed | tf_op | source)
XLA Modules:
  0.0 353.5 jit_solution(1202267567992447423)
XLA Ops:
  7.2 0.0 copy-start
  7.2 2.6 broadcast_in_dim.20
  9.7 11.2 %all-to-all-start = ((bf16[32,16,2048]{2,1,0:T(8,128)(2,1)}), bf16[32,16,2048]{2,1,0:T(8,128)(2,1)}, u32[]{:S(2)}, u32[]{:S(2)}) async-start(bf16[32,16,2048]{2,1,0:T(8,128)(2,1)} %broadcast_in_dim.20), calls=%async_computation | async-start | bytes 4194304 | tf_op jit(solution)/shard_map/all_to_all | solution.py:15
  20.9 0.0 copy-start.5
  20.9 0.0 reduce-scatter.3.cloned.1.call-start
  21.0 6.2 %copy.16 = bf16[1,2,512,2048]{2,3,1,0:T(8,128)(2,1)} copy(bf16[1,2,512,2048]{3,2,1,0:T(8,128)(2,1)} %param.10) | data formatting | bytes 8388608 | tf_op args[4]
  27.2 43.0 %all-to-all-done = bf16[32,16,2048]{2,1,0:T(8,128)(2,1)} async-done(((bf16[32,16,2048]{2,1,0:T(8,128)(2,1)}), bf16[32,16,2048]{2,1,0:T(8,128)(2,1)}, u32[]{:S(2)}, u32[]{:S(2)}) %all-to-all-start) | async-done | bytes 2097184 | tf_op jit(solution)/shard_map/all_to_all | solution.py:15
  70.2 0.0 copy-done
  70.2 0.0 copy-done.5
  70.2 0.0 copy-start.2
  70.2 4.0 %multiply_convert_fusion = (bf16[512,512]{1,0:T(8,128)(2,1)S(1)}, f32[512,512]{1,0:T(8,128)}) fusion(f32[512]{0:T(512)S(1)} %bitcast.103, bf16[512,2048]{1,0:T(8,128)(2,1)} %bitcast.1, bf16[1,2048,512]{2,1,0:T(8,128)(2,1)S(1)} %copy-done), kind=kOutput, calls=%fused_computation.26 | convolution fusion | flops 1074790400 | bytes 5769216 | tf_op jit(solution)/shard_map/dot_general | solution.py:61
  74.2 0.0 copy-done.2
  74.2 2.4 convolution_bitcast_fusion
  76.6 3.8 %copy.17 = f32[2,16,16,4096]{3,2,1,0:T(8,128)} copy(f32[2,16,16,4096]{3,2,0,1:T(8,128)S(1)} %convolution_bitcast_fusion) | data formatting | bytes 16777216 | tf_op jit(solution)/shard_map/transpose | solution.py:41
  80.4 0.0 reduce-scatter.3.cloned.1.call-update
  80.4 0.0 reduce-scatter.5.cloned.1.call-start
  80.5 21.5 %reduce-scatter.3.cloned.1.call-done = f32[16,16,4096]{2,1,0:T(8,128)} async-done(((f32[32,16,4096]{2,1,0:T(8,128)}), f32[16,16,4096]{2,1,0:T(8,128)}) %reduce-scatter.3.cloned.1.call-update) | async-done | bytes 4194320 | tf_op jit(solution)/shard_map/reduce_scatter | solution.py:42
  102.0 0.0 copy-start.3
  102.0 0.0 copy-start.4
  102.0 0.0 reduce-scatter.5.cloned.1.call-update
  102.0 74.1 %reduce-scatter.5.cloned.1.call-done = f32[1,16,4096]{2,1,0:T(8,128)} async-done(((f32[16,16,4096]{2,1,0:T(8,128)}), f32[1,16,4096]{2,1,0:T(8,128)}) %reduce-scatter.5.cloned.1.call-update) | async-done | bytes 262160 | tf_op jit(solution)/shard_map/reduce_scatter | solution.py:43
  176.1 0.9 slice.25
  177.0 3.9 %collective-permute-start = (f32[16,2048]{1,0:T(8,128)S(1)}, f32[16,2048]{1,0:T(8,128)S(1)}, u32[]{:S(2)}, u32[]{:S(2)}) collective-permute-start(f32[16,2048]{1,0:T(8,128)S(1)} %slice.25), channel_id=1, source_target_pairs={{0,32},{32,64},{64,96},{96,128},{128,160},{160,192},{192,224},{1,3... | collective-permute-start | bytes 393224 | tf_op jit(solution)/shard_map/ppermute | solution.py:49
  180.9 3.3 collective-permute-done
  184.2 0.0 copy-done.3
  184.2 0.0 copy-done.4
  184.2 1.6 multiply_reduce_fusion
  185.8 1.3 collective-permute-start.1
  187.1 6.1 %collective-permute-done.1 = bf16[16,2048]{1,0:T(8,128)(2,1)S(1)} collective-permute-done((bf16[16,2048]{1,0:T(8,128)(2,1)S(1)}, bf16[16,2048]{1,0:T(8,128)(2,1)S(1)}, u32[]{:S(2)}, u32[]{:S(2)}) %collective-permute-start.1) | collective-permute-done | bytes 65568 | tf_op jit(solution)/shard_map/ppermute | solution.py:49
  193.1 2.5 stack.17
  195.7 16.4 %all-to-all-start.1 = ((bf16[32,16,2,2048]{3,1,2,0:T(8,128)(2,1)}), bf16[32,16,2,2048]{3,1,2,0:T(8,128)(2,1)}, u32[]{:S(2)}, u32[]{:S(2)}) async-start(bf16[32,16,2,2048]{3,1,2,0:T(8,128)(2,1)} %stack.17), calls=%async_computation.3 | async-start | bytes 8388608 | tf_op jit(solution)/shard_map/all_to_all | solution.py:85
  212.0 11.1 %psum.35 = f32[]{:T(128)} all-reduce(f32[]{:T(128)} %get-tuple-element.20), channel_id=1, replica_groups=mesh['layer_0'=4,'layer_1'=2,'feat_0'=2,'feat_1'=8,'feat_2'=2] {'layer_0'}, use_global_device_ids=true, to_apply=%region_3.0 | all-reduce | flops 1 | bytes 8 | tf_op jit(solution)/shard_map/psum | solution.py:53
  223.1 6.3 %psum.36 = f32[]{:T(128)} all-reduce(f32[]{:T(128)} %psum.35), channel_id=1, replica_groups=mesh['layer_0'=4,'layer_1'=2,'feat_0'=2,'feat_1'=8,'feat_2'=2] {'layer_1'}, use_global_device_ids=true, to_apply=%region_4.0 | all-reduce | flops 1 | bytes 8 | tf_op jit(solution)/shard_map/psum | solution.py:53
  229.4 5.2 %psum.37 = f32[]{:T(128)} all-reduce(f32[]{:T(128)} %psum.36), channel_id=1, replica_groups=mesh['layer_0'=4,'layer_1'=2,'feat_0'=2,'feat_1'=8,'feat_2'=2] {'feat_0'}, use_global_device_ids=true, to_apply=%region_5.0 | all-reduce | flops 1 | bytes 8 | tf_op jit(solution)/shard_map/psum | solution.py:53
  234.6 78.7 %psum.38 = f32[]{:T(128)} all-reduce(f32[]{:T(128)} %psum.37), channel_id=1, replica_groups=mesh['layer_0'=4,'layer_1'=2,'feat_0'=2,'feat_1'=8,'feat_2'=2] {'feat_1'}, use_global_device_ids=true, to_apply=%region_6.0 | all-reduce | flops 1 | bytes 8 | tf_op jit(solution)/shard_map/psum | solution.py:53
  313.3 6.8 %psum.39 = f32[]{:T(128)} all-reduce(f32[]{:T(128)} %psum.38), channel_id=1, replica_groups=mesh['layer_0'=4,'layer_1'=2,'feat_0'=2,'feat_1'=8,'feat_2'=2] {'feat_2'}, use_global_device_ids=true, to_apply=%region_7.0 | all-reduce | flops 1 | bytes 8 | tf_op jit(solution)/shard_map/psum | solution.py:53
  320.7 0.0 all-to-all-done.1
  320.7 0.0 copy-start.1
  320.8 2.7 copy.18
  323.4 1.0 convert_reduce_fusion
  324.4 0.0 copy-done.1
  324.4 1.3 fusion.3
  325.7 2.6 fusion.1
  328.3 0.0 copy-start.6
  328.3 2.6 fusion.2
  330.9 0.0 copy-done.6
  330.9 1.9 convert_reduce_fusion.1
  332.8 4.2 %fusion = bf16[1,2048,512]{1,2,0:T(8,128)(2,1)} fusion(bf16[512,512]{1,0:T(8,128)(2,1)S(1)} %get-tuple-element.25, bf16[512,2048]{1,0:T(8,128)(2,1)} %bitcast.1), kind=kOutput, calls=%fused_computation.6 | convolution fusion | flops 1074790400 | bytes 4718592 | tf_op jit(solution)/shard_map/td,tf->df/dot_general | solution.py:100
  337.0 3.9 %copy.19 = bf16[1,2048,512]{2,1,0:T(8,128)(2,1)} copy(bf16[1,2048,512]{1,2,0:T(8,128)(2,1)} %fusion) | data formatting | bytes 4194304
  340.9 4.6 %maximum_bitcast_fusion = bf16[1,2,512,2048]{3,2,1,0:T(8,128)(2,1)} fusion(bf16[1,512,2048]{2,1,0:T(8,128)(2,1)} %fusion.2, bf16[1,512,2048]{2,1,0:T(8,128)(2,1)} %fusion.1), kind=kLoop, calls=%fused_computation.1 | loop fusion | flops 2097152 | bytes 8388608 | tf_op jit(solution)/shard_map/broadcast_in_dim | solution.py:105
  (1 shorter events, 0.0 us)
Async XLA Ops:
  7.2 63.1 %copy-start = (bf16[1,2048,512]{2,1,0:T(8,128)(2,1)S(1)}, bf16[1,2048,512]{2,1,0:T(8,128)(2,1)}, u32[]{:S(2)}) copy-start(bf16[1,2048,512]{2,1,0:T(8,128)(2,1)} %param.8) | copy-start | bytes 6291460
  9.7 60.5 %all-to-all-start = ((bf16[32,16,2048]{2,1,0:T(8,128)(2,1)}), bf16[32,16,2048]{2,1,0:T(8,128)(2,1)}, u32[]{:S(2)}, u32[]{:S(2)}) async-start(bf16[32,16,2048]{2,1,0:T(8,128)(2,1)} %broadcast_in_dim.20), calls=%async_computation | async-start | bytes 4194304 | tf_op jit(solution)/shard_map/all_to_all | solution.py:15
  20.9 49.3 %copy-start.5 = (f32[1,512]{1,0:T(1,128)S(1)}, f32[1,512]{1,0:T(1,128)}, u32[]{:S(2)}) copy-start(f32[1,512]{1,0:T(1,128)} %param.9) | copy-start | bytes 6148
  20.9 81.0 %reduce-scatter.3.cloned.1.call-start = ((), (), s32[]{:S(2)}) async-start(), calls=%async_computation.4 | async-start | bytes 12582912 | tf_op jit(solution)/shard_map/reduce_scatter | solution.py:42
  70.2 4.0 %copy-start.2 = (bf16[1,2,512,2048]{2,3,1,0:T(8,128)(2,1)S(1)}, bf16[1,2,512,2048]{2,3,1,0:T(8,128)(2,1)}, u32[]{:S(2)}) copy-start(bf16[1,2,512,2048]{2,3,1,0:T(8,128)(2,1)} %copy.16) | copy-start | bytes 12582916
  80.4 95.7 %reduce-scatter.5.cloned.1.call-start = ((), (), s32[]{:S(2)}) async-start(), calls=%async_computation.5 | async-start | bytes 4456448 | tf_op jit(solution)/shard_map/reduce_scatter | solution.py:43
  102.0 82.2 %copy-start.3 = (bf16[1,16,2048]{2,1,0:T(8,128)(2,1)S(1)}, bf16[1,16,2048]{2,1,0:T(8,128)(2,1)}, u32[]{:S(2)}) copy-start(bf16[1,16,2048]{2,1,0:T(8,128)(2,1)} %param.7) | copy-start | bytes 196612
  102.0 82.2 %copy-start.4 = (f32[1,2048]{1,0:T(1,128)S(1)}, f32[1,2048]{1,0:T(1,128)}, u32[]{:S(2)}) copy-start(f32[1,2048]{1,0:T(1,128)} %param.11) | copy-start | bytes 24580
  177.0 7.2 %collective-permute-start = (f32[16,2048]{1,0:T(8,128)S(1)}, f32[16,2048]{1,0:T(8,128)S(1)}, u32[]{:S(2)}, u32[]{:S(2)}) collective-permute-start(f32[16,2048]{1,0:T(8,128)S(1)} %slice.25), channel_id=1, source_target_pairs={{0,32},{32,64},{64,96},{96,128},{128,160},{160,192},{192,224},{1,3... | collective-permute-start | bytes 393224 | tf_op jit(solution)/shard_map/ppermute | solution.py:49
  185.8 7.4 %collective-permute-start.1 = (bf16[16,2048]{1,0:T(8,128)(2,1)S(1)}, bf16[16,2048]{1,0:T(8,128)(2,1)S(1)}, u32[]{:S(2)}, u32[]{:S(2)}) collective-permute-start(bf16[16,2048]{1,0:T(8,128)(2,1)S(1)} %get-tuple-element.21), channel_id=1, source_target_pairs={{32,0},{64,32},{96,64},{128,96},{160,128},{192,160},{224,192},{33,... | collective-permute-start | bytes 196616 | tf_op jit(solution)/shard_map/ppermute | solution.py:49
  195.7 125.1 %all-to-all-start.1 = ((bf16[32,16,2,2048]{3,1,2,0:T(8,128)(2,1)}), bf16[32,16,2,2048]{3,1,2,0:T(8,128)(2,1)}, u32[]{:S(2)}, u32[]{:S(2)}) async-start(bf16[32,16,2,2048]{3,1,2,0:T(8,128)(2,1)} %stack.17), calls=%async_computation.3 | async-start | bytes 8388608 | tf_op jit(solution)/shard_map/all_to_all | solution.py:85
  320.7 3.6 %copy-start.1 = (bf16[1,2,512,2048]{3,2,1,0:T(8,128)(2,1)S(1)}, bf16[1,2,512,2048]{3,2,1,0:T(8,128)(2,1)}, u32[]{:S(2)}) copy-start(bf16[1,2,512,2048]{3,2,1,0:T(8,128)(2,1)} %param.10) | copy-start | bytes 12582916
  328.3 2.6 copy-start.6
Sparse Core Ops, SparseCore 0:
  80.5 21.3 reduce-scatter.2
  104.5 71.4 reduce-scatter.4
